TPU v7x, 256 devices: a whole 4x4x8 slice. The times are simulated.
256 devices in a mesh: ctx: 64 (over x, y_hi, z), ch: 4 (over y_lo, core).
Axes of the slice: x: 4, y: 4 (y_hi: 2, y_lo: 2; y = y_hi * 2 + y_lo), z: 8, core: 2. Of those that a mesh axis runs over, the one named last changes fastest.
Arguments:
- inputs: bfloat16 [32, 16, 8192], P(None, 'ch', 'ctx'), may hold values from -0.0390625 to 0.0390625
- short_filter: float32 [3, 32, 16], P(None, None, 'ch'), may hold values from -3.5 to 3.5
- long_filter: bfloat16 [32, 8192], P(None, 'ctx'), may hold values from -0.15625 to 0.15625
- grad_out: bfloat16 [32, 16, 8192], P(None, 'ch', 'ctx'), may hold values from -6 to 6
Outputs:
- grad_in: bfloat16 [32, 16, 8192], P(None, 'ch', 'ctx')
- grad_long: float32 [32, 8192], P(None, 'ctx')
- grad_short: float32 [3, 32, 16], P(None, None, 'ch')
All inputs are finite; a program needn't handle non-finite values.
Results may differ from a plain program's by a relative error of at most 0.0031.
Values may be sent and summed in bfloat16 or wider, within the bound.
A program may use at most 128 MiB of HBM per device.

v0:
```python
import math
import jax
import jax.numpy as jnp
from jax import lax
from jax.sharding import PartitionSpec as P


def shifted(array, axis, by):
    count = lax.axis_size(axis)
    pairs = [(i, i + by) for i in range(count) if 0 <= i + by < count]
    return lax.ppermute(array, axis, pairs)


def lower_band(matrix, block_len):
    leading = matrix.shape[:-2]
    flattened = matrix.reshape(leading + (2 * block_len * block_len,))
    flattened = jnp.pad(flattened, [(0, 0)] * len(leading) + [(0, block_len)])
    skewed = flattened.reshape(leading + (block_len, 2 * block_len + 1))
    return jnp.sum(skewed[..., :block_len], axis=-2)


def shift_matrix(piece, block_len):
    leading = piece.shape[:-1]
    padded = jnp.pad(piece, [(0, 0)] * len(leading) + [(block_len, block_len + 1)])
    tiled = jnp.broadcast_to(padded[..., None, :], leading + (block_len, 3 * block_len + 1))
    flattened = tiled.reshape(leading + (block_len * (3 * block_len + 1),))[
        ..., : 3 * block_len * block_len
    ]
    skewed = flattened.reshape(leading + (block_len, 3 * block_len))
    return skewed[..., block_len:]


def per_device(inputs, short_filter, long_filter, grad_out):
    tap_count = short_filter.shape[0]
    filter_count, chan_count, shard_len = inputs.shape
    ctx_count = lax.axis_size("ctx")
    my_index = lax.axis_index("ctx")
    total_len = shard_len * ctx_count
    block_len = math.gcd(shard_len, 128)
    own_count = shard_len // block_len
    block_count = total_len // block_len
    margin = tap_count - 1
    edge = shifted(inputs[:, :, shard_len - margin :], "ctx", 1)
    extended = jnp.concatenate([edge, inputs], axis=2).astype(jnp.float32)

    def delayed(offset):
        return lax.slice_in_dim(extended, margin - offset, margin - offset + shard_len, axis=2)

    hidden = sum(
        (short_filter[offset][:, :, None] * delayed(offset) for offset in range(tap_count))
    )
    hidden = hidden.astype(jnp.bfloat16)
    grad_all, filter_all = (
        lax.all_gather(grad_out, "ctx", axis=2, tiled=True),
        lax.all_gather(long_filter, "ctx", axis=1, tiled=True),
    )
    grad_padded = jnp.pad(grad_all, ((0, 0), (0, 0), (0, total_len + block_len)))
    grad_blocks = grad_padded.reshape(filter_count, chan_count, 2 * block_count + 1, block_len)
    filter_blocks = filter_all.reshape(filter_count, block_count, block_len)

    def windows_at(first, count):
        sliced = lax.dynamic_slice_in_dim(grad_blocks, first, count + 1, axis=2)
        return jnp.concatenate([sliced[:, :, :-1], sliced[:, :, 1:]], axis=3)

    block_num = 0
    window = windows_at(my_index * own_count + block_num, block_count)
    banded = jnp.einsum("fkr,fgkj->fgrj", filter_blocks, window, preferred_element_type=jnp.float32)
    pieces = lower_band(banded, block_len)
    following = shifted(pieces[:, :, :margin], "ctx", -1)
    extended_grad = jnp.concatenate([pieces, following], axis=2)
    grad_in = sum(
        (
            short_filter[offset][:, :, None]
            * lax.slice_in_dim(extended_grad, offset, offset + shard_len, axis=2)
            for offset in range(tap_count)
        )
    )
    grad_in = grad_in.astype(jnp.bfloat16)
    local_short = jnp.stack(
        [jnp.sum(pieces * delayed(offset), axis=2) for offset in range(tap_count)]
    )
    grad_short = lax.psum(local_short, "ctx")
    hidden_shards = hidden.reshape(filter_count, chan_count, own_count, block_len)
    count = shard_len * lax.axis_size("ctx")
    first = jnp.int32(0) // block_len
    count_blocks = count // block_len
    block_num = 0
    window = windows_at(my_index * own_count + block_num, count_blocks)
    toeplitz = shift_matrix(hidden_shards[:, :, block_num], block_len)
    term = jnp.einsum("fgkj,fgrj->fkr", window, toeplitz, preferred_element_type=jnp.float32)
    own_lags = lax.psum_scatter(
        term.reshape(filter_count, count).T, "ctx", scatter_dimension=0, tiled=True
    ).T
    grad_long = lax.psum(own_lags, "ch")
    return (grad_in, grad_long, grad_short)


def solution(mesh):
    in_specs = (P(None, "ch", "ctx"), P(None, None, "ch"), P(None, "ctx"), P(None, "ch", "ctx"))
    out_specs = (P(None, "ch", "ctx"), P(None, "ctx"), P(None, None, "ch"))
    return jax.shard_map(
        per_device, mesh=mesh, in_specs=in_specs, out_specs=out_specs, check_vma=False
    )
```

profile of v0, /device:TPU:1, one launch (start us, length us, event | category | flops | bytes accessed | tf_op | source)
XLA Modules:
  0.0 729.9 jit_solution(7096233392741595054)
XLA Ops:
  7.2 0.7 all-gather.2.cloned.1.call-update
  7.9 0.0 reduce-scatter.2.cloned.1.call-start
  7.9 0.8 copy.21
  8.7 0.1 slice.72
  8.8 4.4 collective-permute-start.1
  13.2 158.3 %all_gather.7 = bf16[32,8192]{1,0:T(8,128)(2,1)S(1)} all-gather(bf16[32,128]{1,0:T(8,128)(2,1)} %param.6), channel_id=1, replica_groups=mesh['ctx'=64,'ch'=4] {'ctx'}, dimensions={1}, use_global_device_ids=true | all-gather | bytes 532480 | tf_op jit(solution)/shard_map/all_gather | solution.py:55
  171.5 0.1 copy.39
  171.6 0.7 slice_bitcast_fusion.2
  172.3 4.8 pad.12
  177.1 7.3 %reshape.40 = bf16[32,4,129,128]{3,2,1,0:T(8,128)(2,1)} reshape(bf16[32,4,16512]{2,1,0:T(4,128)(2,1)} %pad.12) | data formatting | bytes 8454144 | tf_op jit(solution)/shard_map/reshape | solution.py:58
  184.5 4.8 constant_dynamic-slice_fusion
  189.3 1.3 copy-done
  190.7 7.1 convolution_bitcast_fusion
  197.8 17.5 %copy.20 = f32[32,4,128,256]{3,2,0,1:T(8,128)} copy(f32[32,4,128,256]{2,3,1,0:T(8,128)} %convolution_bitcast_fusion) | data formatting | bytes 33554432 | tf_op jit(solution)/shard_map/fkr,fgkj->fgrj/transpose | solution.py:67
  215.2 18.2 %reshape.33 = f32[32,4,32768]{2,0,1:T(8,128)} reshape(f32[32,4,128,256]{3,2,0,1:T(8,128)} %copy.20) | data formatting | bytes 33554432 | tf_op jit(solution)/shard_map/reshape | solution.py:16
  233.5 11.4 %pad.13 = f32[32,4,32896]{2,0,1:T(8,128)} pad(f32[32,4,32768]{2,0,1:T(8,128)} %reshape.33, f32[]{:T(128)} %constant.14.clone.1), padding=0_0x0_0x0_128 | pad | bytes 33619972 | tf_op jit(solution)/shard_map/jit(_pad)/pad | solution.py:17
  244.8 26.6 %reshape.34 = f32[32,4,128,257]{3,2,0,1:T(8,128)} reshape(f32[32,4,32896]{2,0,1:T(8,128)} %pad.13) | data formatting | bytes 33685504 | tf_op jit(solution)/shard_map/reshape | solution.py:18
  271.5 4.6 slice_reduce_fusion
  276.0 1.5 collective-permute-start
  277.5 0.1 maximum_convert_fusion
  277.6 3.4 collective-permute-done
  281.1 0.3 multiply_reduce_fusion.2
  281.4 6.1 broadcast_in_dim.2
  287.5 24.6 %reshape.35 = bf16[32,4,49280]{2,0,1:T(8,128)(2,1)} reshape(bf16[32,4,128,385]{3,2,0,1:T(8,128)(2,1)} %broadcast_in_dim.2) | data formatting | bytes 25231360 | tf_op jit(solution)/shard_map/reshape | solution.py:26
  312.0 4.6 slice-done
  316.6 2.7 copy.40
  319.3 4.3 fusion
  323.6 1.6 copy.45
  325.2 0.6 copy.30
  325.9 152.7 %psum.15 = f32[3,32,4]{1,2,0:T(4,128)} all-reduce(f32[3,32,4]{1,2,0:T(4,128)S(1)} %pad_maximum_fusion.4), channel_id=1, replica_groups=mesh['ctx'=64,'ch'=4] {'ctx'}, use_global_device_ids=true, to_apply=%region_6.7 | all-reduce | flops 384 | bytes 3072 | tf_op jit(solution)/shard_map/psum | solution.py:82
  478.6 182.7 %reduce-scatter.2.cloned.1.call-done = f32[128,32]{0,1:T(8,128)} async-done(((f32[8192,32]{0,1:T(8,128)}), f32[128,32]{0,1:T(8,128)}) %reduce-scatter.2.cloned.1.call-update) | async-done | bytes 16400 | tf_op jit(solution)/shard_map/reduce_scatter | solution.py:91
  661.3 61.7 %psum.14 = f32[32,128]{1,0:T(8,128)} all-reduce(f32[32,128]{1,0:T(8,128)} %bitcast.52), channel_id=1, replica_groups=mesh['ctx'=64,'ch'=4] {'ch'}, use_global_device_ids=true, to_apply=%region_2.3 | all-reduce | flops 4096 | bytes 32768 | tf_op jit(solution)/shard_map/psum | solution.py:94
  (8 shorter events, 0.1 us)
Async XLA Ops:
  7.2 165.2 %all-gather.2.cloned.1.call-start = ((), (), s32[]{:S(2)}) async-start(), calls=%async_computation.1 | async-start | bytes 2129920 | tf_op jit(solution)/shard_map/all_gather | solution.py:54
  7.9 653.4 %reduce-scatter.2.cloned.1.call-start = ((), (), s32[]{:S(2)}) async-start(), calls=%async_computation.2 | async-start | bytes 1064960 | tf_op jit(solution)/shard_map/reduce_scatter | solution.py:91
  8.8 268.7 %collective-permute-start.1 = (bf16[32,4,2]{2,0,1:T(8,128)(2,1)S(1)}, bf16[32,4,2]{2,0,1:T(8,128)(2,1)S(1)}, u32[]{:S(2)}, u32[]{:S(2)}) collective-permute-start(bf16[32,4,2]{2,0,1:T(8,128)(2,1)S(1)} %slice.72), channel_id=1, source_target_pairs={{0,4},{4,8},{8,12},{12,16},{16,20},{20,24},{24,28},{28,32},{32,36}... | collective-permute-start | bytes 1544 | tf_op jit(solution)/shard_map/ppermute | solution.py:11
  189.3 1.4 copy-start
  276.0 5.0 collective-permute-start
  312.0 4.6 slice-start
Sparse Core Ops, SparseCore 0:
  11.4 97.2 all-gather.1
  325.4 335.9 reduce-scatter.1
where the time goes:
time: 732 us; the launch traced here: 730 us
  blocking collectives  373 us (51%)
  waiting for transfers between devices  187 us (26%)
  local copies, waits for them, and re-layouts  134 us (18%)
  between operations  14.1 us (2%)
  matrix products  11.5 us (2%)
    reduce_scatter x1, waiting for transfers between devices, per_device(): lax.psum_scatter(term.reshape(filter_count, count).T, 'ctx', scatter_dime...  183 us
    all_gather x1, blocking collectives, per_device(): lax.all_gather(long_filter, 'ctx', axis=1, tiled=True)  158 us
    psum x1, blocking collectives, per_device(): grad_short = lax.psum(local_short, 'ctx')  153 us
    psum x1, blocking collectives, per_device(): grad_long = lax.psum(own_lags, 'ch')  61.7 us
    reshape x1, local copies, waits for them, and re-layouts, lower_band(): skewed = flattened.reshape(leading + (block_len, 2 * block_len + 1))  26.6 us
    reshape x1, local copies, waits for them, and re-layouts, shift_matrix(): tiled.reshape(leading + (block_len * (3 * block_len + 1),))  24.6 us
    reshape x1, local copies, waits for them, and re-layouts, lower_band(): flattened = matrix.reshape(leading + (2 * block_len * block_len,))  18.2 us
    transpose x1, local copies, waits for them, and re-layouts, per_device(): jnp.einsum('fkr,fgkj->fgrj', filter_blocks, window, preferred_element_typ...  17.5 us
  transfers between devices with their start and end apart: 4, of which 2 were waited for; matrix products, arithmetic and copies ran while one was open for 14% of the time, Pallas kernels for 0%

commit v1 on v0

--- a/solution.py
+++ b/solution.py
@@ -52,7 +52,9 @@
     hidden = hidden.astype(jnp.bfloat16)
     grad_all, filter_all = (
         lax.all_gather(grad_out, "ctx", axis=2, tiled=True),
-        lax.all_gather(long_filter, "ctx", axis=1, tiled=True),
+        jnp.concatenate(
+            lax.all_to_all(jnp.stack([long_filter] * lax.axis_size("ctx")), "ctx", 0, 0), axis=1
+        ),
     )
     grad_padded = jnp.pad(grad_all, ((0, 0), (0, 0), (0, total_len + block_len)))
     grad_blocks = grad_padded.reshape(filter_count, chan_count, 2 * block_count + 1, block_len)

time: 732 us -> 659 us (0.900)
  blocking collectives: 373 us -> 220 us
  waiting for transfers between devices: 187 us -> 248 us
  starting transfers between devices: 5.9 us -> 19.6 us
    all_gather x1 -> x0, blocking collectives: 158 us -> none  [per_device(): lax.all_gather(long_filter, 'ctx', axis=1, tiled=True)]
    all_gather x1, waiting for transfers between devices: 0.01 us -> 79 us  [per_device(): lax.all_gather(grad_out, 'ctx', axis=2, tiled=True)]
    reduce_scatter x1, waiting for transfers between devices: 183 us -> 165 us  [per_device(): lax.psum_scatter(term.reshape(filter_count, count).T, 'ctx', scatter_dime...]
    all_to_all x0 -> x1, starting transfers between devices: none -> 15.1 us  [per_device(): lax.all_to_all(jnp.stack([long_filter] * lax.axis_size('ctx')), 'ctx', 0, 0)]
  transfers between devices with their start and end apart: 4 -> 5, of which waited for: 2 -> 3; matrix products, arithmetic and copies ran while one was open for 14% -> 17% of each run, Pallas kernels for 0% -> 0%
where the time goes in v1:
time: 659 us; the launch traced here: 656 us
  waiting for transfers between devices  248 us (38%)
  blocking collectives  220 us (33%)
  local copies, waits for them, and re-layouts  135 us (20%)
  starting transfers between devices  19.6 us (3%)
  matrix products  14.1 us (2%)
  between operations  14.1 us (2%)
    reduce_scatter x1, waiting for transfers between devices, per_device(): lax.psum_scatter(term.reshape(filter_count, count).T, 'ctx', scatter_dime...  165 us
    psum x1, blocking collectives, per_device(): grad_short = lax.psum(local_short, 'ctx')  158 us
    all_gather x1, waiting for transfers between devices, per_device(): lax.all_gather(grad_out, 'ctx', axis=2, tiled=True)  79 us
    psum x1, blocking collectives, per_device(): grad_long = lax.psum(own_lags, 'ch')  61.7 us
    reshape x1, local copies, waits for them, and re-layouts, lower_band(): skewed = flattened.reshape(leading + (block_len, 2 * block_len + 1))  26.6 us
    reshape x1, local copies, waits for them, and re-layouts, shift_matrix(): tiled.reshape(leading + (block_len * (3 * block_len + 1),))  24.6 us
    reshape x1, local copies, waits for them, and re-layouts, lower_band(): flattened = matrix.reshape(leading + (2 * block_len * block_len,))  18.2 us
    transpose x1, local copies, waits for them, and re-layouts, per_device(): jnp.einsum('fkr,fgkj->fgrj', filter_blocks, window, preferred_element_typ...  17.5 us
  transfers between devices with their start and end apart: 5, of which 3 were waited for; matrix products, arithmetic and copies ran while one was open for 17% of the time, Pallas kernels for 0%

profile of v1, /device:TPU:1, one launch (start us, length us, event | category | flops | bytes accessed | tf_op | source)
XLA Modules:
  0.0 656.5 jit_solution(527411935190206058)
XLA Ops:
  7.2 0.7 all-gather.2.cloned.1.call-update
  7.9 1.6 stack.10
  9.5 15.1 %all-to-all-start = ((bf16[64,32,128]{2,1,0:T(8,128)(2,1)}), bf16[64,32,128]{2,1,0:T(8,128)(2,1)S(1)}, u32[]{:S(2)}, u32[]{:S(2)}) async-start(bf16[64,32,128]{2,1,0:T(8,128)(2,1)} %stack.10), calls=%async_computation | async-start | bytes 1048576 | tf_op jit(solution)/shard_map/all_to_all | solution.py:56
  24.6 0.0 reduce-scatter.2.cloned.1.call-start
  24.6 0.8 copy.22
  25.4 0.1 slice.72
  25.5 2.9 collective-permute-start.1
  28.4 0.7 slice_bitcast_fusion.2
  29.1 79.0 %all-gather.2.cloned.1.call-done = bf16[32,4,8192]{2,1,0:T(4,128)(2,1)} async-done(((bf16[32,4,128]{2,1,0:T(4,128)(2,1)}), bf16[32,4,8192]{2,1,0:T(4,128)(2,1)}) %all-gather.2.cloned.1.call-update) | async-done | bytes 2097168 | tf_op jit(solution)/shard_map/all_gather | solution.py:54
  108.1 4.9 pad.12
  113.0 7.3 %reshape.42 = bf16[32,4,129,128]{3,2,1,0:T(8,128)(2,1)} reshape(bf16[32,4,16512]{2,1,0:T(4,128)(2,1)} %pad.12) | data formatting | bytes 8454144 | tf_op jit(solution)/shard_map/reshape | solution.py:60
  120.3 6.2 constant_dynamic-slice_fusion
  126.5 9.8 %convolution_bitcast_fusion = f32[32,4,128,256]{2,3,1,0:T(8,128)} fusion(bf16[32,4,64,128]{3,2,1,0:T(8,128)(2,1)} %get-tuple-element.10, bf16[32,4,64,128]{3,2,1,0:T(8,128)(2,1)S(1)} %get-tuple-element.9, bf16[64,32,128]{2,1,0:T(8,128)(2,1)S(1)} %all-to-all-done), kind=kOutput, calls=%fused_computation | convolution fusion | flops 545259520 | bytes 21495808 | tf_op jit(solution)/shard_map/fkr,fgkj->fgrj/dot_general | solution.py:69
  136.3 17.5 %copy.21 = f32[32,4,128,256]{3,2,0,1:T(8,128)} copy(f32[32,4,128,256]{2,3,1,0:T(8,128)} %convolution_bitcast_fusion) | data formatting | bytes 33554432 | tf_op jit(solution)/shard_map/fkr,fgkj->fgrj/transpose | solution.py:69
  153.8 18.2 %reshape.35 = f32[32,4,32768]{2,0,1:T(8,128)} reshape(f32[32,4,128,256]{3,2,0,1:T(8,128)} %copy.21) | data formatting | bytes 33554432 | tf_op jit(solution)/shard_map/reshape | solution.py:16
  172.0 11.4 %pad.13 = f32[32,4,32896]{2,0,1:T(8,128)} pad(f32[32,4,32768]{2,0,1:T(8,128)} %reshape.35, f32[]{:T(128)} %constant.14.clone.1), padding=0_0x0_0x0_128 | pad | bytes 33619972 | tf_op jit(solution)/shard_map/jit(_pad)/pad | solution.py:17
  183.3 26.6 %reshape.36 = f32[32,4,128,257]{3,2,0,1:T(8,128)} reshape(f32[32,4,32896]{2,0,1:T(8,128)} %pad.13) | data formatting | bytes 33685504 | tf_op jit(solution)/shard_map/reshape | solution.py:18
  210.0 4.6 slice_reduce_fusion
  214.6 1.5 collective-permute-start
  216.1 0.1 maximum_convert_fusion
  216.1 3.4 collective-permute-done
  219.6 0.3 multiply_reduce_fusion.2
  219.9 6.1 broadcast_in_dim.2
  226.0 24.6 %reshape.37 = bf16[32,4,49280]{2,0,1:T(8,128)(2,1)} reshape(bf16[32,4,128,385]{3,2,0,1:T(8,128)(2,1)} %broadcast_in_dim.2) | data formatting | bytes 25231360 | tf_op jit(solution)/shard_map/reshape | solution.py:26
  250.5 4.6 slice-done
  255.1 2.7 copy.40
  257.8 4.3 fusion
  262.1 1.6 copy.49
  263.8 0.6 copy.31
  264.4 158.1 %psum.15 = f32[3,32,4]{1,2,0:T(4,128)} all-reduce(f32[3,32,4]{1,2,0:T(4,128)S(1)} %pad_maximum_fusion.4), channel_id=1, replica_groups=mesh['ctx'=64,'ch'=4] {'ctx'}, use_global_device_ids=true, to_apply=%region_6.7 | all-reduce | flops 384 | bytes 3072 | tf_op jit(solution)/shard_map/psum | solution.py:84
  422.5 165.3 %reduce-scatter.2.cloned.1.call-done = f32[128,32]{0,1:T(8,128)} async-done(((f32[8192,32]{0,1:T(8,128)}), f32[128,32]{0,1:T(8,128)}) %reduce-scatter.2.cloned.1.call-update) | async-done | bytes 16400 | tf_op jit(solution)/shard_map/reduce_scatter | solution.py:93
  587.9 61.7 %psum.14 = f32[32,128]{1,0:T(8,128)} all-reduce(f32[32,128]{1,0:T(8,128)} %bitcast.50), channel_id=1, replica_groups=mesh['ctx'=64,'ch'=4] {'ch'}, use_global_device_ids=true, to_apply=%region_2.3 | all-reduce | flops 4096 | bytes 32768 | tf_op jit(solution)/shard_map/psum | solution.py:96
  (7 shorter events, 0.1 us)
Async XLA Ops:
  7.2 100.9 %all-gather.2.cloned.1.call-start = ((), (), s32[]{:S(2)}) async-start(), calls=%async_computation.2 | async-start | bytes 2129920 | tf_op jit(solution)/shard_map/all_gather | solution.py:54
  9.5 117.0 %all-to-all-start = ((bf16[64,32,128]{2,1,0:T(8,128)(2,1)}), bf16[64,32,128]{2,1,0:T(8,128)(2,1)S(1)}, u32[]{:S(2)}, u32[]{:S(2)}) async-start(bf16[64,32,128]{2,1,0:T(8,128)(2,1)} %stack.10), calls=%async_computation | async-start | bytes 1048576 | tf_op jit(solution)/shard_map/all_to_all | solution.py:56
  24.6 563.3 %reduce-scatter.2.cloned.1.call-start = ((), (), s32[]{:S(2)}) async-start(), calls=%async_computation.3 | async-start | bytes 1064960 | tf_op jit(solution)/shard_map/reduce_scatter | solution.py:93
  25.5 190.6 %collective-permute-start.1 = (bf16[32,4,2]{2,0,1:T(8,128)(2,1)S(1)}, bf16[32,4,2]{2,0,1:T(8,128)(2,1)S(1)}, u32[]{:S(2)}, u32[]{:S(2)}) collective-permute-start(bf16[32,4,2]{2,0,1:T(8,128)(2,1)S(1)} %slice.72), channel_id=1, source_target_pairs={{0,4},{4,8},{8,12},{12,16},{16,20},{20,24},{24,28},{28,32},{32,36}... | collective-permute-start | bytes 1544 | tf_op jit(solution)/shard_map/ppermute | solution.py:11
  214.6 5.0 collective-permute-start
  250.5 4.6 slice-start
Sparse Core Ops, SparseCore 0:
  11.4 96.6 all-gather.1
  263.9 323.9 reduce-scatter.1
